TPU v7x, 32 devices: a whole 2x2x4 slice. The times are simulated.
32 devices in a mesh: ctx: 16 (over z, y, core), fsdp: 2 (over x).
Axes of the slice: x: 2, y: 2, z: 4, core: 2. Of those that a mesh axis runs over, the one named last changes fastest.
Arguments:
- queries: bfloat16 [2, 2048, 2048], P('fsdp', 'ctx'), may hold values from -8 to 8
- keys_values: bfloat16 [2, 2048, 2, 2048], P('fsdp', 'ctx'), may hold values from -8 to 8
- upstream: bfloat16 [2, 2048, 2048], P('fsdp', 'ctx'), may hold values from -6 to 6
- out_weight: bfloat16 [2048, 2048], P('fsdp'), may hold values from -0.125 to 0.125
Outputs:
- grad_queries: bfloat16 [2, 2048, 2048], P('fsdp', 'ctx')
- grad_keys_values: bfloat16 [2, 2048, 2, 2048], P('fsdp', 'ctx')
- grad_weight: float32 [2048, 2048], P(('ctx', 'fsdp'))
All inputs are finite; a program needn't handle non-finite values.
Results may differ from a plain program's by a relative error of at most 0.014.
Values may be sent and summed in bfloat16 or wider, within the bound.
A program may use at most 128 MiB of HBM per device.

v0:
```python
import jax
import jax.numpy as jnp
from jax import lax
from jax.sharding import PartitionSpec as P

HEADS = 16
HEAD_DIM = 128
SPAN = 4
WINDOW = 512
NEGATIVE = -1e30


def passed_along(x, axis, by):
    count = lax.axis_size(axis)
    pairs = [(i, i + by) for i in range(count) if 0 <= i + by < count]
    return lax.ppermute(x, axis, pairs)


def shards(queries, keys_values, upstream, out_weight):
    seq_count, tok_rows, attn_width = queries.shape
    model_width = upstream.shape[2]
    head_count = HEADS
    head_size = HEAD_DIM
    reach_devices = SPAN
    inv_root = head_size ** (-0.5)
    flat_upstream = upstream.reshape(seq_count * tok_rows, model_width)
    grad_attn = jnp.dot(
        flat_upstream,
        lax.all_gather(out_weight, "fsdp", axis=0, tiled=True),
        preferred_element_type=jnp.float32,
    )
    grad_attn = grad_attn.astype(jnp.bfloat16).reshape(seq_count, tok_rows, head_count, head_size)
    moving = keys_values
    earlier = []
    for offset in range(reach_devices):
        moving = passed_along(moving, "ctx", 1)
        earlier = [moving] + earlier
    window_kv = jnp.concatenate(earlier + [keys_values], axis=1)
    key_count = window_kv.shape[1]
    key_heads = window_kv[:, :, 0].reshape(seq_count, key_count, head_count, head_size)
    value_heads = window_kv[:, :, 1].reshape(seq_count, key_count, head_count, head_size)
    query_heads = queries.reshape(seq_count, tok_rows, head_count, head_size)
    ctx_index = lax.axis_index("ctx")
    query_pos = ctx_index * tok_rows + jnp.arange(tok_rows, dtype=jnp.int32)
    key_pos = (ctx_index - reach_devices) * tok_rows + jnp.arange(key_count, dtype=jnp.int32)
    distance = query_pos[:, None] - key_pos[None, :]
    visible = (distance >= 0) & (distance < WINDOW) & (key_pos[None, :] >= 0)
    scores = (
        jnp.einsum("sqhe,skhe->shqk", query_heads, key_heads, preferred_element_type=jnp.float32)
        * inv_root
    )
    scores = jnp.where(visible[None, None], scores, NEGATIVE)
    row_max = jnp.max(scores, axis=-1, keepdims=True)
    lifted = jnp.exp(scores - row_max)
    probability = lifted / jnp.sum(lifted, axis=-1, keepdims=True)
    probs_low = probability.astype(jnp.bfloat16)
    attended = jnp.einsum(
        "shqk,skhe->sqhe", probs_low, value_heads, preferred_element_type=jnp.float32
    ).astype(jnp.bfloat16)
    products = jnp.einsum(
        "sqhe,skhe->shqk", grad_attn, value_heads, preferred_element_type=jnp.float32
    )
    center = jnp.sum(grad_attn.astype(jnp.float32) * attended.astype(jnp.float32), axis=-1)
    center = jnp.swapaxes(center, 1, 2)[:, :, :, None]
    grad_scores = (probability * (products - center)).astype(jnp.bfloat16)
    grad_queries = (
        jnp.einsum("shqk,skhe->sqhe", grad_scores, key_heads, preferred_element_type=jnp.float32)
        * inv_root
    )
    grad_queries = grad_queries.astype(jnp.bfloat16).reshape(seq_count, tok_rows, attn_width)
    grad_keys = (
        jnp.einsum("shqk,sqhe->skhe", grad_scores, query_heads, preferred_element_type=jnp.float32)
        * inv_root
    )
    grad_values = jnp.einsum(
        "shqk,sqhe->skhe", probs_low, grad_attn, preferred_element_type=jnp.float32
    )
    grad_window = jnp.stack(
        [
            grad_keys.reshape(seq_count, key_count, attn_width),
            grad_values.reshape(seq_count, key_count, attn_width),
        ],
        axis=2,
    )
    blocks = [
        grad_window[:, offset * tok_rows : (offset + 1) * tok_rows]
        for offset in range(reach_devices + 1)
    ]
    carried = blocks[0]
    for offset in range(1, reach_devices + 1):
        carried = passed_along(carried, "ctx", -1)
        if offset < reach_devices:
            carried = carried + blocks[offset]
    collected = blocks[reach_devices] + carried
    grad_pairs = collected.astype(jnp.bfloat16)
    flat_attended = attended.reshape(seq_count * tok_rows, attn_width)
    weight_term = lax.dot_general(
        flat_upstream, flat_attended, (((0,), (0,)), ((), ())), preferred_element_type=jnp.float32
    )
    weight_term = lax.optimization_barrier(weight_term.astype(jnp.bfloat16)).astype(jnp.float32)
    ctx_count = lax.axis_size("ctx")
    fsdp_count = lax.axis_size("fsdp")
    own_rows = model_width // (ctx_count * fsdp_count)
    weight_term = weight_term.reshape(ctx_count, fsdp_count, own_rows, attn_width)
    section_one = lax.psum_scatter(weight_term, "ctx", scatter_dimension=0, tiled=True)
    section_two = lax.psum_scatter(section_one, "fsdp", scatter_dimension=1, tiled=True)
    grad_weight = section_two.reshape(own_rows, attn_width)
    return (grad_queries, grad_pairs, grad_weight)


def solution(mesh):
    return jax.shard_map(
        shards,
        mesh=mesh,
        in_specs=(
            P("fsdp", "ctx", None),
            P("fsdp", "ctx", None, None),
            P("fsdp", "ctx", None),
            P("fsdp", None),
        ),
        out_specs=(P("fsdp", "ctx", None), P("fsdp", "ctx", None, None), P(("ctx", "fsdp"), None)),
        check_vma=False,
    )
```

profile of v0, /device:TPU:0, one launch (start us, length us, event | category | flops | bytes accessed | tf_op | source)
XLA Modules:
  0.0 428.0 jit_solution(18424261364848707581)
XLA Ops:
  7.2 0.7 all-gather.2.cloned.1.call-update
  8.0 2.5 copy.23
  10.5 2.5 collective-permute-start
  13.0 2.2 collective-permute-done
  15.2 14.0 %collective-permute-start.1 = (bf16[1,128,2,2048]{1,3,2,0:T(8,128)(2,1)S(1)}, bf16[1,128,2,2048]{1,3,2,0:T(8,128)(2,1)S(1)}, u32[]{:S(2)}, u32[]{:S(2)}) collective-permute-start(bf16[1,128,2,2048]{1,3,2,0:T(8,128)(2,1)S(1)} %collective-permute-done), channel_id=1, source_target_pairs={{0,2},{2,4},{4,6},{6,8},{8,10},{10,12},{12,14},{14,16},{16,18},{18... | collective-permute-start | bytes 3145736 | tf_op jit(solution)/shard_map/ppermute | solution.py:16
  29.2 2.2 collective-permute-done.1
  31.4 1.0 copy-done.10
  32.4 14.8 %collective-permute-start.2 = (bf16[1,128,2,2048]{1,3,2,0:T(8,128)(2,1)S(1)}, bf16[1,128,2,2048]{1,3,2,0:T(8,128)(2,1)}, u32[]{:S(2)}, u32[]{:S(2)}) collective-permute-start(bf16[1,128,2,2048]{1,3,2,0:T(8,128)(2,1)S(1)} %collective-permute-done.1), channel_id=1, source_target_pairs={{0,2},{2,4},{4,6},{6,8},{8,10},{10,12},{12,14},{14,16},{16,18},{18... | collective-permute-start | bytes 3145736 | tf_op jit(solution)/shard_map/ppermute | solution.py:16
  47.2 1.4 collective-permute-done.2
  48.7 14.7 %collective-permute-start.3 = (bf16[1,128,2,2048]{1,3,2,0:T(8,128)(2,1)}, bf16[1,128,2,2048]{1,3,2,0:T(8,128)(2,1)}, u32[]{:S(2)}, u32[]{:S(2)}) collective-permute-start(bf16[1,128,2,2048]{1,3,2,0:T(8,128)(2,1)} %collective-permute-done.2), channel_id=1, source_target_pairs={{0,2},{2,4},{4,6},{6,8},{8,10},{10,12},{12,14},{14,16},{16,18},{18... | collective-permute-start | bytes 3145736 | tf_op jit(solution)/shard_map/ppermute | solution.py:16
  63.4 1.0 copy.51
  64.6 0.3 collective-permute-done.3
  65.0 1.4 constant_dynamic-update-slice_fusion.4
  66.4 1.5 constant_dynamic-update-slice_fusion.3
  67.9 1.5 constant_dynamic-update-slice_fusion.2
  69.3 0.2 constant_dynamic-update-slice_fusion.1
  69.9 2.0 fusion.24
  71.8 5.8 %fusion.25 = (f32[16,128]{1,0:T(8,128)S(1)}, f32[16,128,640]{1,2,0:T(8,128)}) fusion(pred[128,640]{0,1:T(8,128)(4,1)S(1)} %fusion.19, bf16[640,16,128]{0,2,1:T(8,128)(2,1)S(1)} %bitcast.80, bf16[128,16,128]{0,2,1:T(8,128)(2,1)} %bitcast.86), kind=kOutput, calls=%fused_computation.53 | convolution fusion | flops 340787840 | bytes 8478720 | tf_op jit(solution)/shard_map/sub | solution.py:54
  77.6 3.1 fusion.5
  80.8 35.5 %all-gather.2.cloned.1.call-done = bf16[2048,2048]{1,0:T(8,128)(2,1)} async-done(((bf16[1024,2048]{1,0:T(8,128)(2,1)}), bf16[2048,2048]{1,0:T(8,128)(2,1)}) %all-gather.2.cloned.1.call-update) | async-done | bytes 8388624 | tf_op jit(solution)/shard_map/all_gather | solution.py:29
  116.3 5.5 %convolution_convert_fusion = bf16[128,2048]{1,0:T(8,128)(2,1)} fusion(bf16[2048,2048]{1,0:T(8,128)(2,1)} %all-gather.2.cloned.1.call-done, bf16[1,128,2048]{2,1,0:T(8,128)(2,1)S(1)} %copy-done), kind=kOutput, calls=%fused_computation.19 | convolution fusion | flops 1074003968 | bytes 9437184 | tf_op jit(solution)/shard_map/dot_general | solution.py:27
  121.8 2.2 copy.50
  124.0 2.9 multiply_reduce_fusion
  126.8 5.6 %convert_bitcast_fusion = bf16[2048,2048]{0,1:T(8,128)(2,1)} fusion(bf16[128,2048]{0,1:T(8,128)(2,1)S(1)} %bitcast.85, bf16[1,128,2048]{2,1,0:T(8,128)(2,1)S(1)} %copy-done), kind=kOutput, calls=%fused_computation.9 | convolution fusion | flops 1077936128 | bytes 9437184 | tf_op jit(solution)/shard_map/dot_general | solution.py:97
  132.5 13.0 %copy.39 = f32[2048,2048]{1,0:T(8,128)} copy(bf16[2048,2048]{0,1:T(8,128)(2,1)} %convert_bitcast_fusion) | data formatting | bytes 25165824 | tf_op jit(solution)/shard_map/reshape | solution.py:104
  145.8 0.8 copy-done.7
  146.5 1.0 copy.52
  147.5 4.8 %multiply_convert_fusion = bf16[16,128,640]{1,2,0:T(8,128)(2,1)S(1)} fusion(f32[16,128]{1,0:T(8,128)S(1)} %bitcast.91, bf16[128,16,128]{0,2,1:T(8,128)(2,1)} %bitcast.88, bf16[640,16,128]{0,2,1:T(8,128)(2,1)} %bitcast.83, f32[16,128,640]{1,2,0:T(8,128)} %get-tuple-element.12, f32[16,128]{1,0:T(8,128)S(1)} %get-tuple-element.11), kind=kOutput, calls=%fused_computation.12 | convolution fusion | flops 340787200 | bytes 11026432 | tf_op jit(solution)/shard_map/sqhe,skhe->shqk/dot_general | solution.py:60
  152.3 1.5 copy-done.6
  153.8 3.7 multiply_bitcast_fusion
  157.5 6.7 %copy.36 = f32[1,640,16,128]{1,3,2,0:T(8,128)} copy(f32[1,640,16,128]{3,1,2,0:T(8,128)} %multiply_bitcast_fusion) | data formatting | bytes 10485760 | tf_op jit(solution)/shard_map/mul | solution.py:72
  164.2 1.1 fusion.26
  165.2 4.2 copy-done.2
  169.6 1.3 collective-permute-start.4
  170.9 4.8 %collective-permute-done.4 = f32[1,128,2,2048]{1,3,2,0:T(8,128)S(1)} collective-permute-done((f32[1,128,2,2048]{1,3,2,0:T(8,128)S(1)}, f32[1,128,2,2048]{1,3,2,0:T(8,128)S(1)}, u32[]{:S(2)}, u32[]{:S(2)}) %collective-permute-start.4) | collective-permute-done | bytes 2097184 | tf_op jit(solution)/shard_map/ppermute | solution.py:16
  175.7 0.4 fusion.13
  176.1 1.3 collective-permute-start.5
  177.3 36.9 %collective-permute-done.5 = f32[1,128,2,2048]{1,3,2,0:T(8,128)S(1)} collective-permute-done((f32[1,128,2,2048]{1,3,2,0:T(8,128)S(1)}, f32[1,128,2,2048]{1,3,2,0:T(8,128)S(1)}, u32[]{:S(2)}, u32[]{:S(2)}) %collective-permute-start.5) | collective-permute-done | bytes 2097184 | tf_op jit(solution)/shard_map/ppermute | solution.py:16
  214.5 1.6 collective-permute-start.6
  216.1 37.7 %collective-permute-done.6 = f32[1,128,2,2048]{1,3,2,0:T(8,128)S(1)} collective-permute-done((f32[1,128,2,2048]{1,3,2,0:T(8,128)S(1)}, f32[1,128,2,2048]{1,3,2,0:T(8,128)S(1)}, u32[]{:S(2)}, u32[]{:S(2)}) %collective-permute-start.6) | collective-permute-done | bytes 2097184 | tf_op jit(solution)/shard_map/ppermute | solution.py:16
  253.8 1.6 fusion.14
  255.4 1.3 collective-permute-start.7
  256.6 142.5 %reduce-scatter.3.cloned.1.call-done = f32[1,2,64,2048]{3,2,1,0:T(8,128)} async-done(((f32[16,2,64,2048]{3,2,1,0:T(8,128)}), f32[1,2,64,2048]{3,2,1,0:T(8,128)}) %reduce-scatter.3.cloned.1.call-update) | async-done | bytes 1048592 | tf_op jit(solution)/shard_map/reduce_scatter | solution.py:105
  399.2 3.4 fusion.15
  402.6 2.1 copy.40
  404.7 2.4 fusion.10
  407.1 2.0 copy.41
  409.1 12.4 %reduce-scatter.5.cloned.1.call-done = f32[1,1,64,2048]{3,2,1,0:T(8,128)} async-done(((f32[1,2,64,2048]{3,2,1,0:T(8,128)}), f32[1,1,64,2048]{3,2,1,0:T(8,128)}) %reduce-scatter.5.cloned.1.call-update) | async-done | bytes 524304 | tf_op jit(solution)/shard_map/reduce_scatter | solution.py:106
  (33 shorter events, 1.2 us)
Async XLA Ops:
  7.2 109.1 %copy-start = (bf16[1,128,2048]{2,1,0:T(8,128)(2,1)S(1)}, bf16[1,128,2048]{2,1,0:T(8,128)(2,1)}, u32[]{:S(2)}) copy-start(bf16[1,128,2048]{2,1,0:T(8,128)(2,1)} %param.6) | copy-start | bytes 1572868
  7.2 56.2 %copy-start.11 = (bf16[1,128,2048]{2,1,0:T(8,128)(2,1)S(1)}, bf16[1,128,2048]{2,1,0:T(8,128)(2,1)}, u32[]{:S(2)}) copy-start(bf16[1,128,2048]{2,1,0:T(8,128)(2,1)} %param.4) | copy-start | bytes 1572868
  7.2 109.1 %all-gather.2.cloned.1.call-start = ((), (), s32[]{:S(2)}) async-start(), calls=%async_computation.2 | async-start | bytes 12582912 | tf_op jit(solution)/shard_map/all_gather | solution.py:29
  7.9 391.2 %reduce-scatter.3.cloned.1.call-start = ((), (), s32[]{:S(2)}) async-start(), calls=%async_computation.3 | async-start | bytes 17825792 | tf_op jit(solution)/shard_map/reduce_scatter | solution.py:105
  10.5 4.7 %collective-permute-start = (bf16[1,128,2,2048]{1,3,2,0:T(8,128)(2,1)S(1)}, bf16[1,128,2,2048]{1,3,2,0:T(8,128)(2,1)S(1)}, u32[]{:S(2)}, u32[]{:S(2)}) collective-permute-start(bf16[1,128,2,2048]{1,3,2,0:T(8,128)(2,1)S(1)} %copy.23), channel_id=1, source_target_pairs={{0,2},{2,4},{4,6},{6,8},{8,10},{10,12},{12,14},{14,16},{16,18},{18... | collective-permute-start | bytes 3145736 | tf_op jit(solution)/shard_map/ppermute | solution.py:16
  15.2 16.2 %collective-permute-start.1 = (bf16[1,128,2,2048]{1,3,2,0:T(8,128)(2,1)S(1)}, bf16[1,128,2,2048]{1,3,2,0:T(8,128)(2,1)S(1)}, u32[]{:S(2)}, u32[]{:S(2)}) collective-permute-start(bf16[1,128,2,2048]{1,3,2,0:T(8,128)(2,1)S(1)} %collective-permute-done), channel_id=1, source_target_pairs={{0,2},{2,4},{4,6},{6,8},{8,10},{10,12},{12,14},{14,16},{16,18},{18... | collective-permute-start | bytes 3145736 | tf_op jit(solution)/shard_map/ppermute | solution.py:16
  31.4 1.0 copy-start.10
  32.4 16.2 %collective-permute-start.2 = (bf16[1,128,2,2048]{1,3,2,0:T(8,128)(2,1)S(1)}, bf16[1,128,2,2048]{1,3,2,0:T(8,128)(2,1)}, u32[]{:S(2)}, u32[]{:S(2)}) collective-permute-start(bf16[1,128,2,2048]{1,3,2,0:T(8,128)(2,1)S(1)} %collective-permute-done.1), channel_id=1, source_target_pairs={{0,2},{2,4},{4,6},{6,8},{8,10},{10,12},{12,14},{14,16},{16,18},{18... | collective-permute-start | bytes 3145736 | tf_op jit(solution)/shard_map/ppermute | solution.py:16
  48.7 16.3 %collective-permute-start.3 = (bf16[1,128,2,2048]{1,3,2,0:T(8,128)(2,1)}, bf16[1,128,2,2048]{1,3,2,0:T(8,128)(2,1)}, u32[]{:S(2)}, u32[]{:S(2)}) collective-permute-start(bf16[1,128,2,2048]{1,3,2,0:T(8,128)(2,1)} %collective-permute-done.2), channel_id=1, source_target_pairs={{0,2},{2,4},{4,6},{6,8},{8,10},{10,12},{12,14},{14,16},{16,18},{18... | collective-permute-start | bytes 3145736 | tf_op jit(solution)/shard_map/ppermute | solution.py:16
  71.8 5.8 %copy-start.4 = (bf16[1,640,1,2048]{1,3,2,0:T(8,128)(2,1)}, bf16[1,640,1,2048]{1,3,2,0:T(8,128)(2,1)S(1)}, u32[]{:S(2)}) copy-start(bf16[1,640,1,2048]{1,3,2,0:T(8,128)(2,1)S(1)} %get-tuple-element.10) | copy-start | bytes 7864324
  145.5 1.0 copy-start.7
  145.5 276.0 %reduce-scatter.5.cloned.1.call-start = ((), (), s32[]{:S(2)}) async-start(), calls=%async_computation.4 | async-start | bytes 1572864 | tf_op jit(solution)/shard_map/reduce_scatter | solution.py:106
  147.5 6.3 %copy-start.8 = (bf16[1,128,2048]{1,2,0:T(8,128)(2,1)S(1)}, bf16[1,128,2048]{1,2,0:T(8,128)(2,1)}, u32[]{:S(2)}) copy-start(bf16[1,128,2048]{1,2,0:T(8,128)(2,1)} %copy.51) | copy-start | bytes 1572868
  152.3 1.5 copy-start.6
  157.5 6.7 %copy-start.9 = (bf16[128,2048]{0,1:T(8,128)(2,1)S(1)}, bf16[128,2048]{0,1:T(8,128)(2,1)}, u32[]{:S(2)}) copy-start(bf16[128,2048]{0,1:T(8,128)(2,1)} %copy.52) | copy-start | bytes 1572868
  164.2 5.3 %copy-start.2 = (f32[1,640,16,128]{1,3,2,0:T(8,128)S(1)}, f32[1,640,16,128]{1,3,2,0:T(8,128)}, u32[]{:S(2)}) copy-start(f32[1,640,16,128]{1,3,2,0:T(8,128)} %copy.36) | copy-start | bytes 15728644
  165.2 88.5 %copy-start.3 = (f32[16,128,640]{2,1,0:T(8,128)}, f32[16,128,640]{2,1,0:T(8,128)S(1)}, u32[]{:S(2)}) copy-start(f32[16,128,640]{2,1,0:T(8,128)S(1)} %fusion.26) | copy-start | bytes 15728644
  169.6 6.1 %collective-permute-start.4 = (f32[1,128,2,2048]{1,3,2,0:T(8,128)S(1)}, f32[1,128,2,2048]{1,3,2,0:T(8,128)S(1)}, u32[]{:S(2)}, u32[]{:S(2)}) collective-permute-start(f32[1,128,2,2048]{1,3,2,0:T(8,128)S(1)} %fusion.11), channel_id=1, source_target_pairs={{2,0},{4,2},{6,4},{8,6},{10,8},{12,10},{14,12},{16,14},{18,16},{20... | collective-permute-start | bytes 6291464 | tf_op jit(solution)/shard_map/ppermute | solution.py:16
  176.1 38.2 %collective-permute-start.5 = (f32[1,128,2,2048]{1,3,2,0:T(8,128)S(1)}, f32[1,128,2,2048]{1,3,2,0:T(8,128)S(1)}, u32[]{:S(2)}, u32[]{:S(2)}) collective-permute-start(f32[1,128,2,2048]{1,3,2,0:T(8,128)S(1)} %fusion.13), channel_id=1, source_target_pairs={{2,0},{4,2},{6,4},{8,6},{10,8},{12,10},{14,12},{16,14},{18,16},{20... | collective-permute-start | bytes 6291464 | tf_op jit(solution)/shard_map/ppermute | solution.py:16
  214.5 184.7 %copy-start.5 = (bf16[1,640,1,2048]{1,3,2,0:T(8,128)(2,1)S(1)}, bf16[1,640,1,2048]{1,3,2,0:T(8,128)(2,1)}, u32[]{:S(2)}) copy-start(bf16[1,640,1,2048]{1,3,2,0:T(8,128)(2,1)} %copy-done.4) | copy-start | bytes 7864324
  214.5 39.3 %collective-permute-start.6 = (f32[1,128,2,2048]{1,3,2,0:T(8,128)S(1)}, f32[1,128,2,2048]{1,3,2,0:T(8,128)S(1)}, u32[]{:S(2)}, u32[]{:S(2)}) collective-permute-start(f32[1,128,2,2048]{1,3,2,0:T(8,128)S(1)} %fusion.7), channel_id=1, source_target_pairs={{2,0},{4,2},{6,4},{8,6},{10,8},{12,10},{14,12},{16,14},{18,16},{20... | collective-permute-start | bytes 6291464 | tf_op jit(solution)/shard_map/ppermute | solution.py:16
  255.4 149.3 %collective-permute-start.7 = (f32[1,128,2,2048]{1,3,2,0:T(8,128)}, f32[1,128,2,2048]{1,3,2,0:T(8,128)}, u32[]{:S(2)}, u32[]{:S(2)}) collective-permute-start(f32[1,128,2,2048]{1,3,2,0:T(8,128)} %fusion.14), channel_id=1, source_target_pairs={{2,0},{4,2},{6,4},{8,6},{10,8},{12,10},{14,12},{16,14},{18,16},{20... | collective-permute-start | bytes 6291464 | tf_op jit(solution)/shard_map/ppermute | solution.py:16
  402.6 18.9 %copy-start.1 = (bf16[1,128,2048]{2,1,0:T(8,128)(2,1)S(1)}, bf16[1,128,2048]{2,1,0:T(8,128)(2,1)}, u32[]{:S(2)}) copy-start(bf16[1,128,2048]{2,1,0:T(8,128)(2,1)} %param.6) | copy-start | bytes 1572868
Sparse Core Ops, SparseCore 0:
  9.5 106.6 all-gather.1
  145.6 253.4 reduce-scatter.2
  402.0 19.4 reduce-scatter.4
where the time goes:
time: 429 us; the launch traced here: 428 us
  waiting for transfers between devices  277 us (65%)
  starting transfers between devices  51.7 us (12%)
  local copies, waits for them, and re-layouts  44.9 us (10%)
  matrix products  32.7 us (8%)
  between operations  13.9 us (3%)
  other arithmetic  8.09 us (2%)
    reduce_scatter x1, waiting for transfers between devices, shards(): lax.psum_scatter(weight_term, 'ctx', scatter_dimension=0, tiled=True)  143 us
    ppermute x8, waiting for transfers between devices, passed_along(): return lax.ppermute(x, axis, pairs)  85.5 us
    ppermute x8, starting transfers between devices, passed_along(): return lax.ppermute(x, axis, pairs)  51.4 us
    all_gather x1, waiting for transfers between devices, shards(): lax.all_gather(out_weight, 'fsdp', axis=0, tiled=True)  35.5 us
    unnamed x31, local copies, waits for them, and re-layouts  18.8 us
    reshape x1, local copies, waits for them, and re-layouts, shards(): weight_term.reshape(ctx_count, fsdp_count, own_rows, attn_width)  13 us
    reduce_scatter x1, waiting for transfers between devices, shards(): lax.psum_scatter(section_one, 'fsdp', scatter_dimension=1, tiled=True)  12.4 us
  transfers between devices with their start and end apart: 11, of which 10 were waited for; matrix products, arithmetic and copies ran while one was open for 11% of the time, Pallas kernels for 0%

commit v1 on v0

--- a/solution.py
+++ b/solution.py
@@ -8,6 +8,18 @@
 SPAN = 4
 WINDOW = 512
 NEGATIVE = -1e30
+
+
+def doubled_up(x, axis, dim):
+    ways, here, step = (lax.axis_size(axis), lax.axis_index(axis), x.shape[dim])
+    line, have = (x, 1)
+    while have < ways:
+        line = jnp.concatenate(
+            [line, lax.ppermute(line, axis, [(d, (d - have) % ways) for d in range(ways)])],
+            axis=dim,
+        )
+        have = 2 * have
+    return jnp.roll(line, here * step, axis=dim)
 
 
 def passed_along(x, axis, by):
@@ -25,9 +37,7 @@
     inv_root = head_size ** (-0.5)
     flat_upstream = upstream.reshape(seq_count * tok_rows, model_width)
     grad_attn = jnp.dot(
-        flat_upstream,
-        lax.all_gather(out_weight, "fsdp", axis=0, tiled=True),
-        preferred_element_type=jnp.float32,
+        flat_upstream, doubled_up(out_weight, "fsdp", 0), preferred_element_type=jnp.float32
     )
     grad_attn = grad_attn.astype(jnp.bfloat16).reshape(seq_count, tok_rows, head_count, head_size)
     moving = keys_values

time: 429 us -> 399 us (0.930)
  the two profiles are of different devices: /device:TPU:0 before, /device:TPU:5 now
where the time goes in v1:
time: 399 us; the launch traced here: 398 us
  waiting for transfers between devices  270 us (68%)
  local copies, waits for them, and re-layouts  40.7 us (10%)
  matrix products  35.8 us (9%)
  starting transfers between devices  29.1 us (7%)
  between operations  14.3 us (4%)
  other arithmetic  8.39 us (2%)
    ppermute x8, waiting for transfers between devices, passed_along(): return lax.ppermute(x, axis, pairs)  179 us
    ppermute x1, waiting for transfers between devices, doubled_up(): lax.ppermute(line, axis, [(d, (d - have) % ways) for d in range(ways)])  90.8 us
    ppermute x8, starting transfers between devices, passed_along(): return lax.ppermute(x, axis, pairs)  27.6 us
    unnamed x37, local copies, waits for them, and re-layouts  17.4 us
    reshape x1, local copies, waits for them, and re-layouts, shards(): weight_term.reshape(ctx_count, fsdp_count, own_rows, attn_width)  13 us
    dot_general x1, matrix products, shards(): jnp.dot(flat_upstream, doubled_up(out_weight, 'fsdp', 0), preferred_eleme...  11.9 us
  transfers between devices with their start and end apart: 11, of which 9 were waited for; matrix products, arithmetic and copies ran while one was open for 10% of the time, Pallas kernels for 0%

profile of v1, /device:TPU:5, one launch (start us, length us, event | category | flops | bytes accessed | tf_op | source)
XLA Modules:
  0.0 398.0 jit_solution(14290053242129361835)
XLA Ops:
  7.2 2.6 copy.21
  9.8 3.7 collective-permute-start
  13.5 11.7 %collective-permute-done = bf16[1,128,2,2048]{1,3,2,0:T(8,128)(2,1)S(1)} collective-permute-done((bf16[1,128,2,2048]{1,3,2,0:T(8,128)(2,1)S(1)}, bf16[1,128,2,2048]{1,3,2,0:T(8,128)(2,1)S(1)}, u32[]{:S(2)}, u32[]{:S(2)}) %collective-permute-start) | collective-permute-done | bytes 1048608 | tf_op jit(solution)/shard_map/ppermute | solution.py:28
  25.3 5.3 %collective-permute-start.1 = (bf16[1,128,2,2048]{1,3,2,0:T(8,128)(2,1)S(1)}, bf16[1,128,2,2048]{1,3,2,0:T(8,128)(2,1)S(1)}, u32[]{:S(2)}, u32[]{:S(2)}) collective-permute-start(bf16[1,128,2,2048]{1,3,2,0:T(8,128)(2,1)S(1)} %collective-permute-done), channel_id=1, source_target_pairs={{0,2},{2,4},{4,6},{6,8},{8,10},{10,12},{12,14},{14,16},{16,18},{18... | collective-permute-start | bytes 3145736 | tf_op jit(solution)/shard_map/ppermute | solution.py:28
  30.6 11.7 %collective-permute-done.1 = bf16[1,128,2,2048]{1,3,2,0:T(8,128)(2,1)S(1)} collective-permute-done((bf16[1,128,2,2048]{1,3,2,0:T(8,128)(2,1)S(1)}, bf16[1,128,2,2048]{1,3,2,0:T(8,128)(2,1)S(1)}, u32[]{:S(2)}, u32[]{:S(2)}) %collective-permute-start.1) | collective-permute-done | bytes 1048608 | tf_op jit(solution)/shard_map/ppermute | solution.py:28
  42.3 1.0 copy-done.14
  43.2 5.3 %collective-permute-start.2 = (bf16[1,128,2,2048]{1,3,2,0:T(8,128)(2,1)S(1)}, bf16[1,128,2,2048]{1,3,2,0:T(8,128)(2,1)}, u32[]{:S(2)}, u32[]{:S(2)}) collective-permute-start(bf16[1,128,2,2048]{1,3,2,0:T(8,128)(2,1)S(1)} %collective-permute-done.1), channel_id=1, source_target_pairs={{0,2},{2,4},{4,6},{6,8},{8,10},{10,12},{12,14},{14,16},{16,18},{18... | collective-permute-start | bytes 3145736 | tf_op jit(solution)/shard_map/ppermute | solution.py:28
  48.5 11.7 %collective-permute-done.2 = bf16[1,128,2,2048]{1,3,2,0:T(8,128)(2,1)} collective-permute-done((bf16[1,128,2,2048]{1,3,2,0:T(8,128)(2,1)S(1)}, bf16[1,128,2,2048]{1,3,2,0:T(8,128)(2,1)}, u32[]{:S(2)}, u32[]{:S(2)}) %collective-permute-start.2) | collective-permute-done | bytes 1048608 | tf_op jit(solution)/shard_map/ppermute | solution.py:28
  60.3 5.4 %collective-permute-start.3 = (bf16[1,128,2,2048]{1,3,2,0:T(8,128)(2,1)}, bf16[1,128,2,2048]{1,3,2,0:T(8,128)(2,1)}, u32[]{:S(2)}, u32[]{:S(2)}) collective-permute-start(bf16[1,128,2,2048]{1,3,2,0:T(8,128)(2,1)} %collective-permute-done.2), channel_id=1, source_target_pairs={{0,2},{2,4},{4,6},{6,8},{8,10},{10,12},{12,14},{14,16},{16,18},{18... | collective-permute-start | bytes 3145736 | tf_op jit(solution)/shard_map/ppermute | solution.py:28
  65.6 2.0 copy.47
  67.7 0.2 fusion.28
  68.0 9.7 %collective-permute-done.3 = bf16[1,128,2,2048]{1,3,2,0:T(8,128)(2,1)} collective-permute-done((bf16[1,128,2,2048]{1,3,2,0:T(8,128)(2,1)}, bf16[1,128,2,2048]{1,3,2,0:T(8,128)(2,1)}, u32[]{:S(2)}, u32[]{:S(2)}) %collective-permute-start.3) | collective-permute-done | bytes 1048608 | tf_op jit(solution)/shard_map/ppermute | solution.py:28
  77.7 1.4 constant_dynamic-update-slice_fusion.4
  79.1 1.5 constant_dynamic-update-slice_fusion.3
  80.6 1.5 constant_dynamic-update-slice_fusion.2
  82.0 0.2 constant_dynamic-update-slice_fusion.1
  82.3 0.2 constant_dynamic-update-slice_fusion
  82.6 2.0 fusion.35
  84.5 5.8 %fusion.36 = (f32[16,128]{1,0:T(8,128)S(1)}, f32[16,128,640]{1,2,0:T(8,128)}) fusion(pred[128,640]{0,1:T(8,128)(4,1)S(1)} %fusion.28, bf16[640,16,128]{0,2,1:T(8,128)(2,1)S(1)} %bitcast.83, bf16[128,16,128]{0,2,1:T(8,128)(2,1)} %bitcast.88), kind=kOutput, calls=%fused_computation.64 | convolution fusion | flops 340787840 | bytes 8478720 | tf_op jit(solution)/shard_map/sub | solution.py:64
  90.3 3.3 fusion.13
  93.6 0.9 convolution_convert_fusion
  94.5 0.8 copy-done.9
  95.3 5.6 %convert_bitcast_fusion = bf16[2048,2048]{0,1:T(8,128)(2,1)} fusion(bf16[128,2048]{0,1:T(8,128)(2,1)S(1)} %bitcast.87, bf16[1,128,2048]{2,1,0:T(8,128)(2,1)S(1)} %copy-done), kind=kOutput, calls=%fused_computation.16 | convolution fusion | flops 1077936128 | bytes 9437184 | tf_op jit(solution)/shard_map/dot_general | solution.py:107
  100.9 13.0 %copy.35 = f32[2048,2048]{1,0:T(8,128)} copy(bf16[2048,2048]{0,1:T(8,128)(2,1)} %convert_bitcast_fusion) | data formatting | bytes 25165824 | tf_op jit(solution)/shard_map/reshape | solution.py:114
  114.0 0.2 reduce-scatter.5.cloned.1.call-start
  114.2 1.3 collective-permute-start.4
  115.5 90.8 %collective-permute-done.4 = bf16[1024,2048]{1,0:T(8,128)(2,1)} collective-permute-done((bf16[1024,2048]{1,0:T(8,128)(2,1)}, bf16[1024,2048]{1,0:T(8,128)(2,1)}, u32[]{:S(2)}, u32[]{:S(2)}) %collective-permute-start.4) | collective-permute-done | bytes 4194336 | tf_op jit(solution)/shard_map/ppermute | solution.py:18
  206.3 11.9 %fusion.10 = bf16[2048,128]{1,0:T(8,128)(2,1)S(1)} fusion(s32[]{:T(128)S(6)} %select_n.20, bf16[1024,2048]{1,0:T(8,128)(2,1)} %param.7, bf16[1024,2048]{1,0:T(8,128)(2,1)} %collective-permute-done.4, bf16[1,128,2048]{2,1,0:T(8,128)(2,1)S(1)} %copy-done), kind=kOutput, calls=%fused_computation.27 | convolution fusion | flops 1107558400 | bytes 9437188 | tf_op jit(solution)/shard_map/dot_general | solution.py:39
  218.5 4.0 multiply_convert_fusion
  222.5 1.5 copy-done.8
  223.9 3.1 multiply_bitcast_fusion
  227.1 6.1 %copy.33 = f32[1,640,16,128]{1,3,2,0:T(8,128)} copy(f32[1,640,16,128]{3,1,2,0:T(8,128)} %multiply_bitcast_fusion) | data formatting | bytes 10485760 | tf_op jit(solution)/shard_map/mul | solution.py:82
  233.2 1.1 fusion.37
  234.2 2.8 copy-done.2
  237.1 1.9 collective-permute-start.5
  239.1 26.4 %collective-permute-done.5 = f32[1,128,2,2048]{1,3,2,0:T(8,128)S(1)} collective-permute-done((f32[1,128,2,2048]{1,3,2,0:T(8,128)S(1)}, f32[1,128,2,2048]{1,3,2,0:T(8,128)S(1)}, u32[]{:S(2)}, u32[]{:S(2)}) %collective-permute-start.5) | collective-permute-done | bytes 2097184 | tf_op jit(solution)/shard_map/ppermute | solution.py:28
  265.5 0.4 fusion.21
  265.9 1.9 collective-permute-start.6
  267.8 60.0 %collective-permute-done.6 = f32[1,128,2,2048]{1,3,2,0:T(8,128)S(1)} collective-permute-done((f32[1,128,2,2048]{1,3,2,0:T(8,128)S(1)}, f32[1,128,2,2048]{1,3,2,0:T(8,128)S(1)}, u32[]{:S(2)}, u32[]{:S(2)}) %collective-permute-start.6) | collective-permute-done | bytes 2097184 | tf_op jit(solution)/shard_map/ppermute | solution.py:28
  328.0 2.2 collective-permute-start.7
  330.2 26.3 %collective-permute-done.7 = f32[1,128,2,2048]{1,3,2,0:T(8,128)S(1)} collective-permute-done((f32[1,128,2,2048]{1,3,2,0:T(8,128)S(1)}, f32[1,128,2,2048]{1,3,2,0:T(8,128)S(1)}, u32[]{:S(2)}, u32[]{:S(2)}) %collective-permute-start.7) | collective-permute-done | bytes 2097184 | tf_op jit(solution)/shard_map/ppermute | solution.py:28
  356.6 1.6 fusion.22
  358.1 1.9 collective-permute-start.8
  360.1 3.4 fusion.23
  363.5 2.1 copy.36
  365.6 21.1 %collective-permute-done.8 = f32[1,128,2,2048]{1,3,2,0:T(8,128)} collective-permute-done((f32[1,128,2,2048]{1,3,2,0:T(8,128)}, f32[1,128,2,2048]{1,3,2,0:T(8,128)}, u32[]{:S(2)}, u32[]{:S(2)}) %collective-permute-start.8) | collective-permute-done | bytes 2097184 | tf_op jit(solution)/shard_map/ppermute | solution.py:28
  386.7 2.4 fusion.18
  389.1 2.0 copy.37
  (37 shorter events, 0.7 us)
Async XLA Ops:
  7.2 88.2 %copy-start = (bf16[1,128,2048]{2,1,0:T(8,128)(2,1)S(1)}, bf16[1,128,2048]{2,1,0:T(8,128)(2,1)}, u32[]{:S(2)}) copy-start(bf16[1,128,2048]{2,1,0:T(8,128)(2,1)} %param.6) | copy-start | bytes 1572868
  7.2 352.9 %reduce-scatter.3.cloned.1.call-start = ((), (), s32[]{:S(2)}) async-start(), calls=%async_computation.2 | async-start | bytes 17825792 | tf_op jit(solution)/shard_map/reduce_scatter | solution.py:115
  9.8 15.4 %collective-permute-start = (bf16[1,128,2,2048]{1,3,2,0:T(8,128)(2,1)S(1)}, bf16[1,128,2,2048]{1,3,2,0:T(8,128)(2,1)S(1)}, u32[]{:S(2)}, u32[]{:S(2)}) collective-permute-start(bf16[1,128,2,2048]{1,3,2,0:T(8,128)(2,1)S(1)} %copy.21), channel_id=1, source_target_pairs={{0,2},{2,4},{4,6},{6,8},{8,10},{10,12},{12,14},{14,16},{16,18},{18... | collective-permute-start | bytes 3145736 | tf_op jit(solution)/shard_map/ppermute | solution.py:28
  25.3 17.0 %collective-permute-start.1 = (bf16[1,128,2,2048]{1,3,2,0:T(8,128)(2,1)S(1)}, bf16[1,128,2,2048]{1,3,2,0:T(8,128)(2,1)S(1)}, u32[]{:S(2)}, u32[]{:S(2)}) collective-permute-start(bf16[1,128,2,2048]{1,3,2,0:T(8,128)(2,1)S(1)} %collective-permute-done), channel_id=1, source_target_pairs={{0,2},{2,4},{4,6},{6,8},{8,10},{10,12},{12,14},{14,16},{16,18},{18... | collective-permute-start | bytes 3145736 | tf_op jit(solution)/shard_map/ppermute | solution.py:28
  42.3 1.0 copy-start.14
  43.2 17.0 %collective-permute-start.2 = (bf16[1,128,2,2048]{1,3,2,0:T(8,128)(2,1)S(1)}, bf16[1,128,2,2048]{1,3,2,0:T(8,128)(2,1)}, u32[]{:S(2)}, u32[]{:S(2)}) collective-permute-start(bf16[1,128,2,2048]{1,3,2,0:T(8,128)(2,1)S(1)} %collective-permute-done.1), channel_id=1, source_target_pairs={{0,2},{2,4},{4,6},{6,8},{8,10},{10,12},{12,14},{14,16},{16,18},{18... | collective-permute-start | bytes 3145736 | tf_op jit(solution)/shard_map/ppermute | solution.py:28
  60.3 17.4 %collective-permute-start.3 = (bf16[1,128,2,2048]{1,3,2,0:T(8,128)(2,1)}, bf16[1,128,2,2048]{1,3,2,0:T(8,128)(2,1)}, u32[]{:S(2)}, u32[]{:S(2)}) collective-permute-start(bf16[1,128,2,2048]{1,3,2,0:T(8,128)(2,1)} %collective-permute-done.2), channel_id=1, source_target_pairs={{0,2},{2,4},{4,6},{6,8},{8,10},{10,12},{12,14},{14,16},{16,18},{18... | collective-permute-start | bytes 3145736 | tf_op jit(solution)/shard_map/ppermute | solution.py:28
  84.5 5.8 %copy-start.4 = (bf16[1,640,1,2048]{1,3,2,0:T(8,128)(2,1)}, bf16[1,640,1,2048]{1,3,2,0:T(8,128)(2,1)S(1)}, u32[]{:S(2)}) copy-start(bf16[1,640,1,2048]{1,3,2,0:T(8,128)(2,1)S(1)} %get-tuple-element.10) | copy-start | bytes 7864324
  90.3 3.3 copy-start.6
  94.5 0.8 copy-start.9
  114.0 277.1 %reduce-scatter.5.cloned.1.call-start = ((), (), s32[]{:S(2)}) async-start(), calls=%async_computation.3 | async-start | bytes 1572864 | tf_op jit(solution)/shard_map/reduce_scatter | solution.py:116
  114.2 92.1 %collective-permute-start.4 = (bf16[1024,2048]{1,0:T(8,128)(2,1)}, bf16[1024,2048]{1,0:T(8,128)(2,1)}, u32[]{:S(2)}, u32[]{:S(2)}) collective-permute-start(bf16[1024,2048]{1,0:T(8,128)(2,1)} %param.7), channel_id=1, source_target_pairs={{0,1},{1,0},{2,3},{3,2},{4,5},{5,4},{6,7},{7,6},{8,9},{9,8},{10,11... | collective-permute-start | bytes 12582920 | tf_op jit(solution)/shard_map/ppermute | solution.py:18
  115.5 102.8 %copy-start.10 = (bf16[16,128,128]{2,1,0:T(8,128)(2,1)S(1)}, bf16[16,128,128]{2,1,0:T(8,128)(2,1)}, u32[]{:S(2)}) copy-start(bf16[16,128,128]{2,1,0:T(8,128)(2,1)} %copy-done.9) | copy-start | bytes 1572868
  115.5 102.9 %copy-start.7 = (bf16[1,640,1,2048]{1,3,2,0:T(8,128)(2,1)S(1)}, bf16[1,640,1,2048]{1,3,2,0:T(8,128)(2,1)}, u32[]{:S(2)}) copy-start(bf16[1,640,1,2048]{1,3,2,0:T(8,128)(2,1)} %get-tuple-element.9) | copy-start | bytes 7864324
  218.3 4.2 %copy-start.12 = (bf16[2048,128]{1,0:T(8,128)(2,1)}, bf16[2048,128]{1,0:T(8,128)(2,1)S(1)}, u32[]{:S(2)}) copy-start(bf16[2048,128]{1,0:T(8,128)(2,1)S(1)} %fusion.10) | copy-start | bytes 1572868
  218.5 5.5 %copy-start.11 = (bf16[1,128,2048]{1,2,0:T(8,128)(2,1)S(1)}, bf16[1,128,2048]{1,2,0:T(8,128)(2,1)}, u32[]{:S(2)}) copy-start(bf16[1,128,2048]{1,2,0:T(8,128)(2,1)} %copy.47) | copy-start | bytes 1572868
  222.5 1.5 copy-start.8
  227.1 6.1 %copy-start.13 = (bf16[2048,128]{1,0:T(8,128)(2,1)S(1)}, bf16[2048,128]{1,0:T(8,128)(2,1)}, u32[]{:S(2)}) copy-start(bf16[2048,128]{1,0:T(8,128)(2,1)} %copy-done.12) | copy-start | bytes 1572868
  233.2 3.8 copy-start.2
  234.2 122.3 %copy-start.3 = (f32[16,128,640]{2,1,0:T(8,128)}, f32[16,128,640]{2,1,0:T(8,128)S(1)}, u32[]{:S(2)}) copy-start(f32[16,128,640]{2,1,0:T(8,128)S(1)} %fusion.37) | copy-start | bytes 15728644
  237.1 28.4 %collective-permute-start.5 = (f32[1,128,2,2048]{1,3,2,0:T(8,128)S(1)}, f32[1,128,2,2048]{1,3,2,0:T(8,128)S(1)}, u32[]{:S(2)}, u32[]{:S(2)}) collective-permute-start(f32[1,128,2,2048]{1,3,2,0:T(8,128)S(1)} %fusion.19), channel_id=1, source_target_pairs={{2,0},{4,2},{6,4},{8,6},{10,8},{12,10},{14,12},{16,14},{18,16},{20... | collective-permute-start | bytes 6291464 | tf_op jit(solution)/shard_map/ppermute | solution.py:28
  265.9 62.0 %collective-permute-start.6 = (f32[1,128,2,2048]{1,3,2,0:T(8,128)S(1)}, f32[1,128,2,2048]{1,3,2,0:T(8,128)S(1)}, u32[]{:S(2)}, u32[]{:S(2)}) collective-permute-start(f32[1,128,2,2048]{1,3,2,0:T(8,128)S(1)} %fusion.21), channel_id=1, source_target_pairs={{2,0},{4,2},{6,4},{8,6},{10,8},{12,10},{14,12},{16,14},{18,16},{20... | collective-permute-start | bytes 6291464 | tf_op jit(solution)/shard_map/ppermute | solution.py:28
  328.0 32.1 %copy-start.5 = (bf16[1,640,1,2048]{1,3,2,0:T(8,128)(2,1)S(1)}, bf16[1,640,1,2048]{1,3,2,0:T(8,128)(2,1)}, u32[]{:S(2)}) copy-start(bf16[1,640,1,2048]{1,3,2,0:T(8,128)(2,1)} %copy-done.4) | copy-start | bytes 7864324
  328.0 28.5 %collective-permute-start.7 = (f32[1,128,2,2048]{1,3,2,0:T(8,128)S(1)}, f32[1,128,2,2048]{1,3,2,0:T(8,128)S(1)}, u32[]{:S(2)}, u32[]{:S(2)}) collective-permute-start(f32[1,128,2,2048]{1,3,2,0:T(8,128)S(1)} %fusion.15), channel_id=1, source_target_pairs={{2,0},{4,2},{6,4},{8,6},{10,8},{12,10},{14,12},{16,14},{18,16},{20... | collective-permute-start | bytes 6291464 | tf_op jit(solution)/shard_map/ppermute | solution.py:28
  358.1 28.6 %collective-permute-start.8 = (f32[1,128,2,2048]{1,3,2,0:T(8,128)}, f32[1,128,2,2048]{1,3,2,0:T(8,128)}, u32[]{:S(2)}, u32[]{:S(2)}) collective-permute-start(f32[1,128,2,2048]{1,3,2,0:T(8,128)} %fusion.22), channel_id=1, source_target_pairs={{2,0},{4,2},{6,4},{8,6},{10,8},{12,10},{14,12},{16,14},{18,16},{20... | collective-permute-start | bytes 6291464 | tf_op jit(solution)/shard_map/ppermute | solution.py:28
  363.5 27.6 %copy-start.1 = (bf16[1,128,2048]{2,1,0:T(8,128)(2,1)S(1)}, bf16[1,128,2048]{2,1,0:T(8,128)(2,1)}, u32[]{:S(2)}) copy-start(bf16[1,128,2048]{2,1,0:T(8,128)(2,1)} %param.6) | copy-start | bytes 1572868
Sparse Core Ops, SparseCore 0:
  114.1 200.3 reduce-scatter.2
  360.2 19.8 reduce-scatter.4
